TPU v7x, 256 devices: a whole 4x4x8 slice. The times are simulated.
256 devices in a mesh: row: 16 (over z, y_lo), col: 16 (over x, y_hi, core).
Axes of the slice: x: 4, y: 4 (y_hi: 2, y_lo: 2; y = y_hi * 2 + y_lo), z: 8, core: 2. Of those that a mesh axis runs over, the one named last changes fastest.
Arguments:
- raw: int32 [32768, 4096], P('col', 'row'), may hold values from -128 to 127
- taps: int32 [16, 128], replicated, may hold values from -256 to 256
Outputs:
- visibility: bfloat16 [32, 4096, 2, 4096], P(None, 'row', None, 'col')
All inputs are finite; a program needn't handle non-finite values.
Results may differ from a plain program's by a relative error of at most 0.0056.
Values may be sent and summed in bfloat16 or wider, within the bound.
A program may use at most 128 MiB of HBM per device.

v0:
```python
import math
import jax
import jax.numpy as jnp
from jax import lax
from jax.sharding import PartitionSpec as P

CHANNELS = 32
TRANSFORM = 128
TAPS = 16
SPECTRA_DEV = 16
BLOCKS = 2


def from_behind(block, axis, distance):
    devices = range(lax.axis_size(axis))
    route = [(i - distance, i) for i in devices if i - distance in devices]
    return lax.ppermute(block, axis, route)


def swap_block(block):
    size = lax.axis_size("row")
    route = [(i * size + j, j * size + i) for i in range(size) for j in range(size)]
    return lax.ppermute(block, ("row", "col"), route)


def dft_table():
    sample = jnp.arange(TRANSFORM, dtype=jnp.int32)[:, None]
    channel = jnp.arange(1, CHANNELS + 1, dtype=jnp.int32)[None, :]
    phase = (sample * channel % TRANSFORM).astype(jnp.float32) * (2.0 * math.pi / TRANSFORM)
    return jnp.concatenate([jnp.cos(phase), -jnp.sin(phase)], axis=1)


def channelize(extended, taps, count):
    coeffs = taps.astype(jnp.float32)
    weighted = jnp.zeros((count, TRANSFORM, extended.shape[2]), jnp.float32)
    for offset in range(TAPS):
        start = TAPS - 1 - offset
        weighted = weighted + coeffs[offset][None, :, None] * extended[
            start : start + count
        ].astype(jnp.float32)
    scale = 1.0 / (8192.0 * math.sqrt(TAPS * TRANSFORM))
    spectra = (
        jnp.einsum("sni,nk->ksi", weighted, dft_table(), precision=lax.Precision.HIGHEST) * scale
    )
    return spectra.reshape(2, CHANNELS, count, extended.shape[2]).astype(jnp.bfloat16)


def correlate(row_block, column_block):
    spectra_all = row_block.shape[2]
    width = spectra_all // BLOCKS
    total = None
    for block in range(BLOCKS):
        left = jnp.concatenate(
            [
                row_block[0, :, block * width : (block + 1) * width],
                row_block[1, :, block * width : (block + 1) * width],
            ],
            axis=1,
        )
        real_part = column_block[0, :, block * width : (block + 1) * width]
        imag_part = column_block[1, :, block * width : (block + 1) * width]
        right = jnp.concatenate(
            [
                jnp.concatenate([real_part, imag_part], axis=1),
                jnp.concatenate([-imag_part, real_part], axis=1),
            ],
            axis=2,
        )
        term = lax.dot_general(
            left, right, (((1,), (1,)), ((0,), (0,))), preferred_element_type=jnp.float32
        )
        if block == 0:
            total = term
        else:
            summed = total + term
            total = summed
    result = (total * (1.0 / spectra_all)).astype(jnp.bfloat16)
    return result.reshape(CHANNELS, row_block.shape[3], 2, column_block.shape[3])


def body(raw, taps):
    frames = raw.astype(jnp.bfloat16).reshape(SPECTRA_DEV, TRANSFORM, raw.shape[1])
    rim_frames = frames[SPECTRA_DEV - (TAPS - 1) :]
    earlier = from_behind(rim_frames, "col", 1)
    extended = jnp.concatenate([earlier, frames], axis=0)
    pieces = channelize(extended, taps, SPECTRA_DEV)
    swapped = swap_block(pieces)
    row_block = lax.all_gather(pieces, "col", axis=2, tiled=True)
    column_block = lax.all_gather(swapped, "row", axis=2, tiled=True)
    return correlate(row_block, column_block)


def solution(mesh):
    placed = (P("col", "row"), P())
    return jax.shard_map(
        body, mesh=mesh, in_specs=placed, out_specs=P(None, "row", None, "col"), check_vma=False
    )
```

profile of v0, /device:TPU:1, one launch (start us, length us, event | category | flops | bytes accessed | tf_op | source)
XLA Modules:
  0.0 380.7 jit_solution(359038543877682941)
XLA Ops:
  6.5 0.0 copy-start.5
  6.5 0.0 all-gather.3.cloned.1.call-start
  6.5 1.8 convert_element_type.70
  8.3 0.1 slice.166
  8.4 6.2 %collective-permute-start = (bf16[15,128,256]{2,1,0:T(8,128)(2,1)S(1)}, bf16[15,128,256]{2,1,0:T(8,128)(2,1)S(1)}, u32[]{:S(2)}, u32[]{:S(2)}) collective-permute-start(bf16[15,128,256]{2,1,0:T(8,128)(2,1)S(1)} %bitcast.61), channel_id=1, source_target_pairs={{0,1},{1,2},{2,3},{3,4},{4,5},{5,6},{6,7},{7,8},{8,9},{9,10},{10,1... | collective-permute-start | bytes 2949128 | tf_op jit(solution)/shard_map/ppermute | solution.py:17
  14.6 0.0 copy-done.5
  14.7 0.2 fusion.128
  14.8 10.8 %collective-permute-done = bf16[15,128,256]{2,1,0:T(8,128)(2,1)S(1)} collective-permute-done((bf16[15,128,256]{2,1,0:T(8,128)(2,1)S(1)}, bf16[15,128,256]{2,1,0:T(8,128)(2,1)S(1)}, u32[]{:S(2)}, u32[]{:S(2)}) %collective-permute-start) | collective-permute-done | bytes 983072 | tf_op jit(solution)/shard_map/ppermute | solution.py:17
  25.6 6.0 %fusion.72 = bf16[64,16,256]{2,0,1:T(8,128)(2,1)} fusion(bf16[16,128,256]{2,1,0:T(8,128)(2,1)S(1)} %bitcast.54, bf16[15,128,256]{2,1,0:T(8,128)(2,1)S(1)} %collective-permute-done, f32[128]{0:T(128)S(1)} %get-tuple-element.16, f32[128]{0:T(128)S(1)} %get-tuple-element.17, f32[128]{0:T(128)S(1)} %get-tuple-element.18, f32[128]{0:T(128)S(1)} %get-tuple-element.19, ...), kind=kOutput, calls=%fused_computation.103 | convolution fusion | flops 451420160 | bytes 2596864 | tf_op jit(solution)/shard_map/sni,nk->ksi/dot_general | solution.py:43
  31.6 0.0 all-gather.3.cloned.1.call-update
  31.6 0.0 all-gather.5.cloned.1.call-start
  31.7 1.3 copy.7
  33.0 1.9 collective-permute-start.1
  34.9 8.7 %collective-permute-done.1 = bf16[2,32,16,256]{3,2,1,0:T(8,128)(2,1)S(1)} collective-permute-done((bf16[2,32,16,256]{3,2,1,0:T(8,128)(2,1)S(1)}, bf16[2,32,16,256]{3,2,1,0:T(8,128)(2,1)S(1)}, u32[]{:S(2)}, u32[]{:S(2)}) %collective-permute-start.1) | collective-permute-done | bytes 524320 | tf_op jit(solution)/shard_map/ppermute | solution.py:23
  43.7 0.0 copy-start.4
  43.7 0.8 copy-done.4
  44.5 0.0 all-gather.5.cloned.1.call-update
  44.5 101.8 %all-gather.3.cloned.1.call-done = bf16[2,32,256,256]{3,1,0,2:T(8,128)(2,1)} async-done(((bf16[2,32,16,256]{3,1,0,2:T(8,128)(2,1)}), bf16[2,32,256,256]{3,1,0,2:T(8,128)(2,1)}) %all-gather.3.cloned.1.call-update) | async-done | bytes 8388624 | tf_op jit(solution)/shard_map/all_gather | solution.py:88
  146.3 5.8 %fusion.135 = (bf16[1,32,128,256]{3,1,0,2:T(8,128)(2,1)}, bf16[1,32,128,256]{3,1,0,2:T(8,128)(2,1)}, bf16[1,32,128,256]{3,1,0,2:T(8,128)(2,1)}, bf16[1,32,128,256]{3,1,0,2:T(8,128)(2,1)S(1)}) fusion(bf16[2,32,256,256]{3,1,0,2:T(8,128)(2,1)} %all-gather.3.cloned.1.call-done), kind=kLoop, calls=%fused_computation.173 | loop fusion | bytes 16777216 | tf_op jit(solution)/shard_map/slice | solution.py:55
  152.1 4.5 %copy.12 = bf16[1,32,128,256]{2,3,1,0:T(8,128)(2,1)} copy(bf16[1,32,128,256]{3,1,0,2:T(8,128)(2,1)} %get-tuple-element.5) | data formatting | bytes 4194304
  156.7 4.6 %copy.11 = bf16[1,32,128,256]{2,3,1,0:T(8,128)(2,1)} copy(bf16[1,32,128,256]{3,1,0,2:T(8,128)(2,1)} %get-tuple-element.6) | data formatting | bytes 4194304
  161.2 4.5 %copy.10 = bf16[1,32,128,256]{2,3,1,0:T(8,128)(2,1)} copy(bf16[1,32,128,256]{3,1,0,2:T(8,128)(2,1)} %get-tuple-element.7) | data formatting | bytes 4194304
  165.8 3.1 copy.13
  168.9 159.2 %all-gather.5.cloned.1.call-done = bf16[2,32,256,256]{3,2,1,0:T(8,128)(2,1)} async-done(((bf16[2,32,16,256]{3,2,1,0:T(8,128)(2,1)}), bf16[2,32,256,256]{3,2,1,0:T(8,128)(2,1)}) %all-gather.5.cloned.1.call-update) | async-done | bytes 8388624 | tf_op jit(solution)/shard_map/all_gather | solution.py:89
  328.1 0.0 copy-start
  328.1 4.0 %fusion.134 = (bf16[32,128,256]{2,1,0:T(8,128)(2,1)}, bf16[32,128,256]{2,1,0:T(8,128)(2,1)S(1)}) fusion(bf16[2,32,256,256]{3,2,1,0:T(8,128)(2,1)} %all-gather.5.cloned.1.call-done), kind=kLoop, calls=%fused_computation.172 | loop fusion | flops 2097152 | bytes 8388608 | tf_op jit(solution)/shard_map/neg | solution.py:65
  332.1 1.4 copy-done
  333.5 0.0 copy-start.2
  333.5 0.0 copy-start.3
  333.5 4.2 %slice_bitcast_fusion = (bf16[32,128,256]{2,1,0:T(8,128)(2,1)}, bf16[32,128,256]{2,1,0:T(8,128)(2,1)}, bf16[32,128,256]{2,1,0:T(8,128)(2,1)}, bf16[32,128,256]{2,1,0:T(8,128)(2,1)}) fusion(bf16[2,32,256,256]{3,2,1,0:T(8,128)(2,1)S(1)} %copy-done), kind=kLoop, calls=%fused_computation.50 | loop fusion | bytes 16777216 | tf_op jit(solution)/shard_map/squeeze | solution.py:61
  337.7 0.0 copy-done.2
  337.7 0.8 copy-done.3
  338.5 0.0 copy-start.1
  338.5 9.2 %fusion = f32[32,256,512]{2,1,0:T(8,128)} fusion(bf16[32,128,256]{2,1,0:T(8,128)(2,1)} %get-tuple-element.12, bf16[32,128,256]{2,1,0:T(8,128)(2,1)S(1)} %get-tuple-element.14, bf16[32,128,256]{2,1,0:T(8,128)(2,1)} %get-tuple-element.11, bf16[32,128,256]{1,2,0:T(8,128)(2,1)S(1)} %bitcast.57, bf16[32,128,256]{1,2,0:T(8,128)(2,1)S(1)} %bitcast.58), kind=kOutput, calls=%fused_computation.1 | convolution fusion | flops 2189426688 | bytes 27262976 | tf_op jit(solution)/shard_map/dot_general | solution.py:69
  347.8 0.0 copy-done.1
  347.8 13.7 %multiply_convert_fusion = bf16[32,256,512]{2,1,0:T(8,128)(2,1)} fusion(f32[32,256,512]{2,1,0:T(8,128)} %fusion, bf16[32,128,256]{2,1,0:T(8,128)(2,1)} %get-tuple-element.10, bf16[32,128,256]{2,1,0:T(8,128)(2,1)} %get-tuple-element.13, bf16[32,128,256]{2,1,0:T(8,128)(2,1)} %get-tuple-element.9, bf16[32,128,256]{1,2,0:T(8,128)(2,1)} %bitcast.56, ...), kind=kOutput, calls=%fused_computation | convolution fusion | flops 2202009600 | bytes 35651584 | tf_op jit(solution)/shard_map/dot_general | solution.py:69
  361.4 12.5 %reshape.30 = bf16[32,256,2,256]{3,2,1,0:T(2,128)(2,1)} reshape(bf16[32,256,512]{2,1,0:T(8,128)(2,1)} %multiply_convert_fusion) | data formatting | bytes 16777216 | tf_op jit(solution)/shard_map/reshape | solution.py:78
  (3 shorter events, 0.0 us)
Async XLA Ops:
  6.5 8.1 %copy-start.5 = (s32[16,128]{1,0:T(8,128)S(1)}, s32[16,128]{1,0:T(8,128)}, u32[]{:S(2)}) copy-start(s32[16,128]{1,0:T(8,128)} %param.3) | copy-start | bytes 24580
  6.5 139.8 %all-gather.3.cloned.1.call-start = ((), (), s32[]{:S(2)}) async-start(), calls=%async_computation | async-start | bytes 8912896 | tf_op jit(solution)/shard_map/all_gather | solution.py:88
  8.4 17.2 %collective-permute-start = (bf16[15,128,256]{2,1,0:T(8,128)(2,1)S(1)}, bf16[15,128,256]{2,1,0:T(8,128)(2,1)S(1)}, u32[]{:S(2)}, u32[]{:S(2)}) collective-permute-start(bf16[15,128,256]{2,1,0:T(8,128)(2,1)S(1)} %bitcast.61), channel_id=1, source_target_pairs={{0,1},{1,2},{2,3},{3,4},{4,5},{5,6},{6,7},{7,8},{8,9},{9,10},{10,1... | collective-permute-start | bytes 2949128 | tf_op jit(solution)/shard_map/ppermute | solution.py:17
  31.6 296.5 %all-gather.5.cloned.1.call-start = ((), (), s32[]{:S(2)}) async-start(), calls=%async_computation.1 | async-start | bytes 8912896 | tf_op jit(solution)/shard_map/all_gather | solution.py:89
  33.0 10.7 %collective-permute-start.1 = (bf16[2,32,16,256]{3,2,1,0:T(8,128)(2,1)S(1)}, bf16[2,32,16,256]{3,2,1,0:T(8,128)(2,1)S(1)}, u32[]{:S(2)}, u32[]{:S(2)}) collective-permute-start(bf16[2,32,16,256]{3,2,1,0:T(8,128)(2,1)S(1)} %copy.7), channel_id=1, source_target_pairs={{0,0},{1,16},{2,32},{3,48},{4,64},{5,80},{6,96},{7,112},{8,128},{9... | collective-permute-start | bytes 1572872 | tf_op jit(solution)/shard_map/ppermute | solution.py:23
  43.7 0.8 copy-start.4
  328.1 5.4 %copy-start = (bf16[2,32,256,256]{3,2,1,0:T(8,128)(2,1)S(1)}, bf16[2,32,256,256]{3,2,1,0:T(8,128)(2,1)}, u32[]{:S(2)}) copy-start(bf16[2,32,256,256]{3,2,1,0:T(8,128)(2,1)} %all-gather.5.cloned.1.call-done) | copy-start | bytes 25165828
  333.5 4.2 %copy-start.2 = (bf16[1,32,128,256]{2,3,1,0:T(8,128)(2,1)S(1)}, bf16[1,32,128,256]{2,3,1,0:T(8,128)(2,1)}, u32[]{:S(2)}) copy-start(bf16[1,32,128,256]{2,3,1,0:T(8,128)(2,1)} %copy.11) | copy-start | bytes 6291460
  333.5 5.0 %copy-start.3 = (bf16[1,32,128,256]{2,3,1,0:T(8,128)(2,1)S(1)}, bf16[1,32,128,256]{2,3,1,0:T(8,128)(2,1)}, u32[]{:S(2)}) copy-start(bf16[1,32,128,256]{2,3,1,0:T(8,128)(2,1)} %copy.10) | copy-start | bytes 6291460
  338.5 9.2 %copy-start.1 = (bf16[1,32,128,256]{2,3,1,0:T(8,128)(2,1)S(1)}, bf16[1,32,128,256]{2,3,1,0:T(8,128)(2,1)}, u32[]{:S(2)}) copy-start(bf16[1,32,128,256]{2,3,1,0:T(8,128)(2,1)} %copy.12) | copy-start | bytes 6291460
Sparse Core Ops, SparseCore 0:
  31.7 114.5 all-gather.2
  148.1 179.9 all-gather.4
where the time goes:
time: 381 us
  waiting for transfers between devices  281 us (74%)
  local copies, waits for them, and re-layouts  43.7 us (11%)
  matrix products  28.9 us (8%)
  between operations  13.5 us (4%)
  starting transfers between devices  8.18 us (2%)
  other arithmetic  5.91 us (2%)
    all_gather x1, waiting for transfers between devices, body(): column_block = lax.all_gather(swapped, 'row', axis=2, tiled=True)  159 us
    all_gather x1, waiting for transfers between devices, body(): row_block = lax.all_gather(pieces, 'col', axis=2, tiled=True)  102 us
    dot_general x2, matrix products, correlate(): lax.dot_general(left, right, (((1,), (1,)), ((0,), (0,))), preferred_elem...  22.9 us
    unnamed x16, local copies, waits for them, and re-layouts  19.8 us
    reshape x1, local copies, waits for them, and re-layouts, correlate(): result.reshape(CHANNELS, row_block.shape[3], 2, column_block.shape[3])  12.5 us
    ppermute x1, waiting for transfers between devices, from_behind(): return lax.ppermute(block, axis, route)  10.8 us
    ppermute x1, waiting for transfers between devices, swap_block(): return lax.ppermute(block, ('row', 'col'), route)  8.74 us
  transfers between devices with their start and end apart: 4, of which 4 were waited for; matrix products, arithmetic and copies ran while one was open for 6% of the time, Pallas kernels for 0%

commit v1 on v0

--- a/solution.py
+++ b/solution.py
@@ -86,7 +86,10 @@
     pieces = channelize(extended, taps, SPECTRA_DEV)
     swapped = swap_block(pieces)
     row_block = lax.all_gather(pieces, "col", axis=2, tiled=True)
-    column_block = lax.all_gather(swapped, "row", axis=2, tiled=True)
+    block_last = lax.axis_size("row")
+    mixed_arr = jnp.stack(block_last * [swapped], 0)
+    tile_out = lax.all_to_all(mixed_arr, "row", 0, 0)
+    column_block = jnp.concatenate(tile_out, axis=2)
     return correlate(row_block, column_block)
 
 

time: 381 us -> 351 us (0.921)
  waiting for transfers between devices: 281 us -> 189 us
  starting transfers between devices: 8.18 us -> 57.8 us
  local copies, waits for them, and re-layouts: 43.7 us -> 54.1 us
    all_gather x1 -> x0, waiting for transfers between devices: 159 us -> none  [body(): column_block = lax.all_gather(swapped, 'row', axis=2, tiled=True)]
    all_to_all x0 -> x1, waiting for transfers between devices: none -> 118 us  [body(): tile_out = lax.all_to_all(mixed_arr, 'row', 0, 0)]
    all_gather x1, waiting for transfers between devices: 102 us -> 51 us  [body(): row_block = lax.all_gather(pieces, 'col', axis=2, tiled=True)]
    all_to_all x0 -> x1, starting transfers between devices: none -> 49.7 us  [body(): tile_out = lax.all_to_all(mixed_arr, 'row', 0, 0)]
    reshape x0 -> x1, local copies, waits for them, and re-layouts: none -> 8.01 us  [body(): column_block = jnp.concatenate(tile_out, axis=2)]
    another operation x0 -> x1, local copies, waits for them, and re-layouts: none -> 4.35 us  [body(): mixed_arr = jnp.stack(block_last * [swapped], 0)]
  transfers between devices with their start and end apart: 4 -> 4, of which waited for: 4 -> 4; matrix products, arithmetic and copies ran while one was open for 6% -> 8% of each run, Pallas kernels for 0% -> 0%
where the time goes in v1:
time: 351 us; the launch traced here: 348 us
  waiting for transfers between devices  189 us (54%)
  starting transfers between devices  57.8 us (16%)
  local copies, waits for them, and re-layouts  54.1 us (15%)
  matrix products  28.1 us (8%)
  between operations  13.5 us (4%)
  other arithmetic  5.91 us (2%)
    all_to_all x1, waiting for transfers between devices, body(): tile_out = lax.all_to_all(mixed_arr, 'row', 0, 0)  118 us
    all_gather x1, waiting for transfers between devices, body(): row_block = lax.all_gather(pieces, 'col', axis=2, tiled=True)  51 us
    all_to_all x1, starting transfers between devices, body(): tile_out = lax.all_to_all(mixed_arr, 'row', 0, 0)  49.7 us
    dot_general x2, matrix products, correlate(): lax.dot_general(left, right, (((1,), (1,)), ((0,), (0,))), preferred_elem...  22.9 us
    unnamed x16, local copies, waits for them, and re-layouts  18.9 us
    reshape x1, local copies, waits for them, and re-layouts, correlate(): result.reshape(CHANNELS, row_block.shape[3], 2, column_block.shape[3])  12.5 us
    ppermute x1, waiting for transfers between devices, from_behind(): return lax.ppermute(block, axis, route)  10.8 us
    ppermute x1, waiting for transfers between devices, swap_block(): return lax.ppermute(block, ('row', 'col'), route)  8.7 us
  transfers between devices with their start and end apart: 4, of which 4 were waited for; matrix products, arithmetic and copies ran while one was open for 8% of the time, Pallas kernels for 0%

profile of v1, /device:TPU:1, one launch (start us, length us, event | category | flops | bytes accessed | tf_op | source)
XLA Modules:
  0.0 348.0 jit_solution(13776900160269548349)
XLA Ops:
  6.5 0.0 copy-start.5
  6.5 0.0 all-gather.2.cloned.1.call-start
  6.5 1.8 convert_element_type.70
  8.3 0.1 slice.166
  8.4 6.2 %collective-permute-start = (bf16[15,128,256]{2,1,0:T(8,128)(2,1)S(1)}, bf16[15,128,256]{2,1,0:T(8,128)(2,1)S(1)}, u32[]{:S(2)}, u32[]{:S(2)}) collective-permute-start(bf16[15,128,256]{2,1,0:T(8,128)(2,1)S(1)} %bitcast.63), channel_id=1, source_target_pairs={{0,1},{1,2},{2,3},{3,4},{4,5},{5,6},{6,7},{7,8},{8,9},{9,10},{10,1... | collective-permute-start | bytes 2949128 | tf_op jit(solution)/shard_map/ppermute | solution.py:17
  14.6 0.0 copy-done.5
  14.7 0.2 fusion.128
  14.8 10.8 %collective-permute-done = bf16[15,128,256]{2,1,0:T(8,128)(2,1)S(1)} collective-permute-done((bf16[15,128,256]{2,1,0:T(8,128)(2,1)S(1)}, bf16[15,128,256]{2,1,0:T(8,128)(2,1)S(1)}, u32[]{:S(2)}, u32[]{:S(2)}) %collective-permute-start) | collective-permute-done | bytes 983072 | tf_op jit(solution)/shard_map/ppermute | solution.py:17
  25.6 5.2 %fusion.72 = bf16[64,16,256]{2,0,1:T(8,128)(2,1)S(1)} fusion(bf16[16,128,256]{2,1,0:T(8,128)(2,1)S(1)} %bitcast.58, bf16[15,128,256]{2,1,0:T(8,128)(2,1)S(1)} %collective-permute-done, f32[128]{0:T(128)S(1)} %get-tuple-element.16, f32[128]{0:T(128)S(1)} %get-tuple-element.17, f32[128]{0:T(128)S(1)} %get-tuple-element.18, f32[128]{0:T(128)S(1)} %get-tuple-element.19, ...), kind=kOutput, calls=%fused_computation.103 | convolution fusion | flops 451420160 | bytes 2596864 | tf_op jit(solution)/shard_map/sni,nk->ksi/dot_general | solution.py:43
  30.8 0.0 copy-start.4
  30.8 1.9 collective-permute-start.1
  32.7 0.0 copy-done.4
  32.7 0.0 all-gather.2.cloned.1.call-update
  32.8 8.7 %collective-permute-done.1 = bf16[2,32,16,256]{3,1,0,2:T(8,128)(2,1)S(1)} collective-permute-done((bf16[2,32,16,256]{3,1,0,2:T(8,128)(2,1)S(1)}, bf16[2,32,16,256]{3,1,0,2:T(8,128)(2,1)S(1)}, u32[]{:S(2)}, u32[]{:S(2)}) %collective-permute-start.1) | collective-permute-done | bytes 524320 | tf_op jit(solution)/shard_map/ppermute | solution.py:23
  41.5 0.3 copy.7
  41.8 4.3 %stack.2 = bf16[16,2,32,16,256]{4,3,2,1,0:T(8,128)(2,1)} broadcast(bf16[2,32,16,256]{3,2,1,0:T(8,128)(2,1)S(1)} %copy.7), dimensions={1,2,3,4} | broadcast | bytes 8912896 | tf_op jit(solution)/shard_map/stack | solution.py:90
  46.1 49.7 %all-to-all-start = ((bf16[16,2,32,16,256]{4,3,2,1,0:T(8,128)(2,1)}), bf16[16,2,32,16,256]{4,3,2,1,0:T(8,128)(2,1)}, u32[]{:S(2)}, u32[]{:S(2)}) async-start(bf16[16,2,32,16,256]{4,3,2,1,0:T(8,128)(2,1)} %stack.2), calls=%async_computation | async-start | bytes 16777216 | tf_op jit(solution)/shard_map/all_to_all | solution.py:91
  95.8 51.0 %all-gather.2.cloned.1.call-done = bf16[2,32,256,256]{3,1,0,2:T(8,128)(2,1)} async-done(((bf16[2,32,16,256]{3,1,0,2:T(8,128)(2,1)}), bf16[2,32,256,256]{3,1,0,2:T(8,128)(2,1)}) %all-gather.2.cloned.1.call-update) | async-done | bytes 8388624 | tf_op jit(solution)/shard_map/all_gather | solution.py:88
  146.9 5.8 %fusion.135 = (bf16[1,32,128,256]{3,1,0,2:T(8,128)(2,1)}, bf16[1,32,128,256]{3,1,0,2:T(8,128)(2,1)}, bf16[1,32,128,256]{3,1,0,2:T(8,128)(2,1)}, bf16[1,32,128,256]{3,1,0,2:T(8,128)(2,1)S(1)}) fusion(bf16[2,32,256,256]{3,1,0,2:T(8,128)(2,1)} %all-gather.2.cloned.1.call-done), kind=kLoop, calls=%fused_computation.173 | loop fusion | bytes 16777216 | tf_op jit(solution)/shard_map/slice | solution.py:55
  152.6 4.5 %copy.13 = bf16[1,32,128,256]{2,3,1,0:T(8,128)(2,1)} copy(bf16[1,32,128,256]{3,1,0,2:T(8,128)(2,1)} %get-tuple-element.5) | data formatting | bytes 4194304
  157.2 4.5 %copy.12 = bf16[1,32,128,256]{2,3,1,0:T(8,128)(2,1)} copy(bf16[1,32,128,256]{3,1,0,2:T(8,128)(2,1)} %get-tuple-element.6) | data formatting | bytes 4194304
  161.7 4.5 %copy.11 = bf16[1,32,128,256]{2,3,1,0:T(8,128)(2,1)} copy(bf16[1,32,128,256]{3,1,0,2:T(8,128)(2,1)} %get-tuple-element.7) | data formatting | bytes 4194304
  166.2 3.1 copy.14
  169.3 118.1 %all-to-all-done = bf16[16,2,32,16,256]{4,3,2,1,0:T(8,128)(2,1)} async-done(((bf16[16,2,32,16,256]{4,3,2,1,0:T(8,128)(2,1)}), bf16[16,2,32,16,256]{4,3,2,1,0:T(8,128)(2,1)}, u32[]{:S(2)}, u32[]{:S(2)}) %all-to-all-start) | async-done | bytes 8388640 | tf_op jit(solution)/shard_map/all_to_all | solution.py:91
  287.4 8.0 %copy.8 = bf16[2,32,16,16,256]{4,3,2,1,0:T(8,128)(2,1)} copy(bf16[2,32,16,16,256]{4,3,1,0,2:T(8,128)(2,1)} %bitcast.22) | data formatting | bytes 16777216 | tf_op jit(solution)/shard_map/reshape | solution.py:92
  295.4 0.0 copy-start
  295.4 4.0 %fusion.134 = (bf16[32,128,256]{2,1,0:T(8,128)(2,1)}, bf16[32,128,256]{2,1,0:T(8,128)(2,1)S(1)}) fusion(bf16[2,32,256,256]{3,2,1,0:T(8,128)(2,1)} %bitcast.56), kind=kLoop, calls=%fused_computation.172 | loop fusion | flops 2097152 | bytes 8388608 | tf_op jit(solution)/shard_map/neg | solution.py:65
  299.4 1.4 copy-done
  300.8 0.0 copy-start.2
  300.8 0.0 copy-start.3
  300.8 4.2 %slice_bitcast_fusion = (bf16[32,128,256]{2,1,0:T(8,128)(2,1)}, bf16[32,128,256]{2,1,0:T(8,128)(2,1)}, bf16[32,128,256]{2,1,0:T(8,128)(2,1)}, bf16[32,128,256]{2,1,0:T(8,128)(2,1)}) fusion(bf16[2,32,256,256]{3,2,1,0:T(8,128)(2,1)S(1)} %bitcast.57), kind=kLoop, calls=%fused_computation.50 | loop fusion | bytes 16777216 | tf_op jit(solution)/shard_map/squeeze | solution.py:61
  304.9 0.0 copy-done.2
  304.9 0.8 copy-done.3
  305.8 0.0 copy-start.1
  305.8 9.2 %fusion = f32[32,256,512]{2,1,0:T(8,128)} fusion(bf16[32,128,256]{2,1,0:T(8,128)(2,1)} %get-tuple-element.12, bf16[32,128,256]{2,1,0:T(8,128)(2,1)S(1)} %get-tuple-element.14, bf16[32,128,256]{2,1,0:T(8,128)(2,1)} %get-tuple-element.11, bf16[32,128,256]{1,2,0:T(8,128)(2,1)S(1)} %bitcast.61, bf16[32,128,256]{1,2,0:T(8,128)(2,1)S(1)} %bitcast.62), kind=kOutput, calls=%fused_computation.1 | convolution fusion | flops 2189426688 | bytes 27262976 | tf_op jit(solution)/shard_map/dot_general | solution.py:69
  315.0 0.0 copy-done.1
  315.0 13.6 %multiply_convert_fusion = bf16[32,256,512]{2,1,0:T(8,128)(2,1)} fusion(f32[32,256,512]{2,1,0:T(8,128)} %fusion, bf16[32,128,256]{2,1,0:T(8,128)(2,1)} %get-tuple-element.10, bf16[32,128,256]{2,1,0:T(8,128)(2,1)} %get-tuple-element.13, bf16[32,128,256]{2,1,0:T(8,128)(2,1)} %get-tuple-element.9, bf16[32,128,256]{1,2,0:T(8,128)(2,1)} %bitcast.60, ...), kind=kOutput, calls=%fused_computation | convolution fusion | flops 2202009600 | bytes 35651584 | tf_op jit(solution)/shard_map/dot_general | solution.py:69
  328.7 12.5 %reshape.40 = bf16[32,256,2,256]{3,2,1,0:T(2,128)(2,1)} reshape(bf16[32,256,512]{2,1,0:T(8,128)(2,1)} %multiply_convert_fusion) | data formatting | bytes 16777216 | tf_op jit(solution)/shard_map/reshape | solution.py:78
  (3 shorter events, 0.0 us)
Async XLA Ops:
  6.5 8.1 %copy-start.5 = (s32[16,128]{1,0:T(8,128)S(1)}, s32[16,128]{1,0:T(8,128)}, u32[]{:S(2)}) copy-start(s32[16,128]{1,0:T(8,128)} %param.3) | copy-start | bytes 24580
  6.5 140.3 %all-gather.2.cloned.1.call-start = ((), (), s32[]{:S(2)}) async-start(), calls=%async_computation.1 | async-start | bytes 8912896 | tf_op jit(solution)/shard_map/all_gather | solution.py:88
  8.4 17.2 %collective-permute-start = (bf16[15,128,256]{2,1,0:T(8,128)(2,1)S(1)}, bf16[15,128,256]{2,1,0:T(8,128)(2,1)S(1)}, u32[]{:S(2)}, u32[]{:S(2)}) collective-permute-start(bf16[15,128,256]{2,1,0:T(8,128)(2,1)S(1)} %bitcast.63), channel_id=1, source_target_pairs={{0,1},{1,2},{2,3},{3,4},{4,5},{5,6},{6,7},{7,8},{8,9},{9,10},{10,1... | collective-permute-start | bytes 2949128 | tf_op jit(solution)/shard_map/ppermute | solution.py:17
  30.8 1.9 copy-start.4
  30.8 10.7 %collective-permute-start.1 = (bf16[2,32,16,256]{3,1,0,2:T(8,128)(2,1)S(1)}, bf16[2,32,16,256]{3,1,0,2:T(8,128)(2,1)S(1)}, u32[]{:S(2)}, u32[]{:S(2)}) collective-permute-start(bf16[2,32,16,256]{3,1,0,2:T(8,128)(2,1)S(1)} %bitcast.64), channel_id=1, source_target_pairs={{0,0},{1,16},{2,32},{3,48},{4,64},{5,80},{6,96},{7,112},{8,128},{9... | collective-permute-start | bytes 1572872 | tf_op jit(solution)/shard_map/ppermute | solution.py:23
  46.1 241.3 %all-to-all-start = ((bf16[16,2,32,16,256]{4,3,2,1,0:T(8,128)(2,1)}), bf16[16,2,32,16,256]{4,3,2,1,0:T(8,128)(2,1)}, u32[]{:S(2)}, u32[]{:S(2)}) async-start(bf16[16,2,32,16,256]{4,3,2,1,0:T(8,128)(2,1)} %stack.2), calls=%async_computation | async-start | bytes 16777216 | tf_op jit(solution)/shard_map/all_to_all | solution.py:91
  295.4 5.4 %copy-start = (bf16[2,32,16,16,256]{4,3,2,1,0:T(8,128)(2,1)S(1)}, bf16[2,32,16,16,256]{4,3,2,1,0:T(8,128)(2,1)}, u32[]{:S(2)}) copy-start(bf16[2,32,16,16,256]{4,3,2,1,0:T(8,128)(2,1)} %copy.8) | copy-start | bytes 25165828
  300.8 4.2 %copy-start.2 = (bf16[1,32,128,256]{2,3,1,0:T(8,128)(2,1)S(1)}, bf16[1,32,128,256]{2,3,1,0:T(8,128)(2,1)}, u32[]{:S(2)}) copy-start(bf16[1,32,128,256]{2,3,1,0:T(8,128)(2,1)} %copy.12) | copy-start | bytes 6291460
  300.8 5.0 %copy-start.3 = (bf16[1,32,128,256]{2,3,1,0:T(8,128)(2,1)S(1)}, bf16[1,32,128,256]{2,3,1,0:T(8,128)(2,1)}, u32[]{:S(2)}) copy-start(bf16[1,32,128,256]{2,3,1,0:T(8,128)(2,1)} %copy.11) | copy-start | bytes 6291460
  305.8 9.2 %copy-start.1 = (bf16[1,32,128,256]{2,3,1,0:T(8,128)(2,1)S(1)}, bf16[1,32,128,256]{2,3,1,0:T(8,128)(2,1)}, u32[]{:S(2)}) copy-start(bf16[1,32,128,256]{2,3,1,0:T(8,128)(2,1)} %copy.13) | copy-start | bytes 6291460
Sparse Core Ops, SparseCore 0:
  32.9 113.9 all-gather.1
